TPU v7x, 128 devices: a whole 4x4x4 slice. The times are simulated.
128 devices in a mesh: req: 4 (over z), seq: 32 (over y, x, core).
Axes of the slice: x: 4, y: 4, z: 4, core: 2. Of those that a mesh axis runs over, the one named last changes fastest.
Arguments:
- prompts: bfloat16 [24, 2048, 1024], P('req', 'seq'), may hold values from -6 to 6
- perm: int32 [24], replicated, may hold values from 0 to 23, each once
- lengths: int32 [24], replicated, may hold values from 512 to 2048, as said below
- norm_attn: float32 [1024], replicated, may hold values from 0.25 to 1.75
- norm_mlp: float32 [1024], replicated, may hold values from 0.25 to 1.75
- qkv_train: float32 [1024, 3072], P('seq', 'req'), may hold values from -0.1875 to 0.1875
- qkv_bias: float32 [3072], replicated, may hold values from -3 to 3
- out_train: float32 [1024, 1024], P('seq', 'req'), may hold values from -0.1875 to 0.1875
- gateup_train: float32 [1024, 5632], P('seq', 'req'), may hold values from -0.1875 to 0.1875
- down_train: float32 [2816, 1024], P('seq', 'req'), may hold values from -0.109375 to 0.109375
Outputs:
- states: bfloat16 [24, 2048, 1024], P('req', 'seq')
- key_cache: bfloat16 [24, 2048, 1024], P('req', 'seq')
- value_cache: bfloat16 [24, 2048, 1024], P('req', 'seq')
Inputs may be any that keep to these rules, and one draw needn't show every extreme that they name: Valid lengths; some prompt has exactly 2048 and some exactly 512.
All inputs are finite; a program needn't handle non-finite values.
Results may differ from a plain program's by a relative error of at most 0.0085.
Values may be sent and summed in bfloat16 or wider, within the bound.
A program may use at most 192 MiB of HBM per device.

v0:
```python
import jax
import jax.numpy as jnp
from jax import lax
from jax.sharding import PartitionSpec as P

HEADS = 16
HD = 64


def rms_scale(rows, gain):
    rows = rows.astype(jnp.float32)
    return rows * lax.rsqrt(jnp.mean(rows * rows, axis=-1, keepdims=True) + 1e-06) * gain


def rotate(block, positions):
    half = HD // 2
    count = block.shape[0]
    freqs = jnp.power(1000000.0, -2.0 * jnp.arange(half).astype(jnp.float32) / HD)
    angle = positions[:, None] * freqs[None, :]
    cosine = jnp.cos(angle)[:, None, :]
    sine = jnp.sin(angle)[:, None, :]
    heads = block.reshape(count, -1, HD)
    first = heads[:, :, :half]
    second = heads[:, :, half:]
    turned = jnp.concatenate(
        [first * cosine - second * sine, second * cosine + first * sine], axis=-1
    )
    return turned.reshape(count, -1)


def apply(inputs, gathered):
    return jnp.concatenate(
        [jnp.dot(inputs, gathered[r], preferred_element_type=jnp.float32) for r in range(gathered.shape[0])],
        axis=1,
    )


def attend(items):
    query, keys, values = items
    length = query.shape[2]
    block = min(512, length)
    scale = HD ** (-0.5)
    pieces = []
    for start in range(0, length, block):
        q_block = query[:, :, start : start + block]
        scores = (
            jnp.einsum("bnid,bnjd->bnij", q_block, keys, preferred_element_type=jnp.float32) * scale
        )
        causal = jnp.arange(length)[None, :] <= (start + jnp.arange(block))[:, None]
        scores = jnp.where(causal[None, None], scores, -1e30)
        top = jnp.max(scores, axis=-1, keepdims=True)
        expo = jnp.exp(scores - top)
        probs = (expo / jnp.sum(expo, axis=-1, keepdims=True)).astype(jnp.bfloat16)
        out = jnp.einsum("bnij,bnjd->bnid", probs, values, preferred_element_type=jnp.float32)
        pieces.append(out.astype(jnp.bfloat16))
    return jnp.concatenate(pieces, axis=2)


def gather_weights(piece, rows=None):
    piece = piece.astype(jnp.bfloat16)
    if rows is not None and rows != piece.shape[0]:
        piece = jnp.pad(piece, ((0, rows - piece.shape[0]), (0, 0)))
    whole = lax.all_gather(piece[None], ("req", "seq"), axis=0, tiled=True)
    return whole.reshape(lax.axis_size("req"), -1, piece.shape[1])


def local(
    prompts,
    perm,
    lengths,
    norm_attn,
    norm_mlp,
    qkv_train,
    qkv_bias,
    out_train,
    gateup_train,
    down_train,
):
    count = prompts.shape[0]
    tok = prompts.shape[1]
    width = prompts.shape[2]
    groups = lax.axis_size("seq")

    w_qkv = gather_weights(qkv_train)
    down_rows = down_train.shape[0]
    padded_rows = -(-down_rows // 16) * 16
    width_rows = out_train.shape[0]
    down_piece = jnp.pad(down_train.astype(jnp.bfloat16), ((0, padded_rows - down_rows), (0, 0)))
    side = jnp.concatenate(
        [out_train.astype(jnp.bfloat16), gateup_train.astype(jnp.bfloat16), down_piece.reshape(width_rows, -1)],
        axis=1,
    )
    rest = lax.all_gather(side[None], ("req", "seq"), axis=0, tiled=True)
    blocks = lax.axis_size("req")
    cut_out = out_train.shape[1]
    cut_gu = cut_out + gateup_train.shape[1]
    w_out = rest[:, :, :cut_out].reshape(blocks, -1, cut_out)
    w_gu = rest[:, :, cut_out:cut_gu].reshape(blocks, -1, gateup_train.shape[1])
    w_down = rest[:, :, cut_gu:].reshape(blocks, -1, down_train.shape[1])

    places = lax.axis_index("seq") * tok + jnp.arange(tok, dtype=jnp.int32)
    positions = jnp.tile(places, count).astype(jnp.float32)

    initials = lax.axis_index("req") * count + jnp.arange(count, dtype=jnp.int32)
    own_len = jnp.take(lengths, initials)
    valid = (places[None, :] < own_len[:, None]).astype(jnp.float32).reshape(count * tok, 1)
    rows = prompts.reshape(count * tok, width)
    normed = rms_scale(rows, norm_attn).astype(jnp.bfloat16)
    qkv = apply(normed, w_qkv) + qkv_bias
    query = rotate(qkv[:, :width], positions).astype(jnp.bfloat16)
    keys = rotate(qkv[:, width : 2 * width], positions).astype(jnp.bfloat16)
    values = qkv[:, 2 * width :].astype(jnp.bfloat16)
    per_device = count * HEADS // groups

    def to_pairs(array):
        paired = array.reshape(count, tok, HEADS, HD).transpose(0, 2, 1, 3)
        return paired.reshape(groups, per_device, tok, HD)

    gathered = attend(
        (
            lax.all_to_all(to_pairs(query), "seq", split_axis=0, concat_axis=2, tiled=True),
            lax.all_to_all(to_pairs(keys), "seq", split_axis=0, concat_axis=2, tiled=True),
            lax.all_to_all(to_pairs(values), "seq", split_axis=0, concat_axis=2, tiled=True),
        )
    )
    returned = lax.all_to_all(gathered, "seq", split_axis=2, concat_axis=0, tiled=True)
    attended = (
        returned.reshape(count, HEADS, tok, HD).transpose(0, 2, 1, 3).reshape(count * tok, width)
    )
    mid = rows.astype(jnp.float32) + apply(attended, w_out)
    normed2 = rms_scale(mid, norm_mlp).astype(jnp.bfloat16)
    both = apply(normed2, w_gu)
    half = both.shape[1] // 2
    hidden = (jax.nn.silu(both[:, :half]) * both[:, half:]).astype(jnp.bfloat16)
    hidden = jnp.pad(
        hidden.reshape(count * tok, groups, down_rows), ((0, 0), (0, 0), (0, padded_rows - down_rows))
    ).reshape(count * tok, -1)
    states = (
        ((mid + apply(hidden, w_down)) * valid).astype(jnp.bfloat16).reshape(count, tok, width)
    )

    later, _ = lax.optimization_barrier((prompts, qkv))
    everyone = lax.all_gather(later, "req", axis=0, tiled=True)
    everyone, _ = lax.optimization_barrier((everyone, hidden))
    chosen = jnp.take(perm, initials)
    dealt = jnp.take(everyone, chosen, axis=0).reshape(count * tok, width)
    slot_len = jnp.take(lengths, chosen)
    keep = (places[None, :] < slot_len[:, None]).astype(jnp.bfloat16).reshape(count * tok, 1)
    normed_d = rms_scale(dealt, norm_attn).astype(jnp.bfloat16)
    qkv_d = apply(normed_d, w_qkv) + qkv_bias
    keys_d = rotate(qkv_d[:, width : 2 * width], positions).astype(jnp.bfloat16)
    values_d = qkv_d[:, 2 * width :].astype(jnp.bfloat16)
    key_cache = (keys_d * keep).reshape(count, tok, width)
    value_cache = (values_d * keep).reshape(count, tok, width)
    return (states, key_cache, value_cache)


def solution(mesh):
    placed = (
        P("req", "seq", None),
        P(),
        P(),
        P(),
        P(),
        P("seq", "req"),
        P(),
        P("seq", "req"),
        P("seq", "req"),
        P("seq", "req"),
    )
    return jax.shard_map(
        local,
        mesh=mesh,
        in_specs=placed,
        out_specs=(P("req", "seq", None), P("req", "seq", None), P("req", "seq", None)),
        check_vma=False,
    )
```

profile of v0, /device:TPU:1, one launch (start us, length us, event | category | flops | bytes accessed | tf_op | source)
XLA Modules:
  0.0 414.4 jit_solution(1283903514809066979)
XLA Ops:
  11.6 72.0 %all-gather.8.cloned.1.call-done = bf16[4096,768]{1,0:T(8,128)(2,1)} async-done(((bf16[32,768]{1,0:T(8,128)(2,1)}), bf16[4096,768]{1,0:T(8,128)(2,1)}) %all-gather.8.cloned.1.call-update) | async-done | bytes 6291472 | tf_op jit(solution)/shard_map/all_gather | solution.py:63
  89.7 2.8 maximum_add_fusion
  101.3 4.2 %fusion.82 = (f32[384,1024]{1,0:T(8,128)}, f32[384,1024]{1,0:T(8,128)}) fusion(f32[384,3072]{1,0:T(8,128)} %maximum_add_fusion), kind=kLoop, calls=%fused_computation.149 | loop fusion | bytes 6291456 | tf_op jit(solution)/shard_map/slice | solution.py:110
  107.4 3.0 copy.75
  112.4 3.0 copy.78
  115.3 3.9 reshape.920
  119.2 5.4 %all-to-all-start.2 = ((bf16[32,2,6144]{2,1,0:T(2,128)(2,1)}), bf16[32,2,6144]{2,1,0:T(2,128)(2,1)S(1)}, u32[]{:S(2)}, u32[]{:S(2)}) async-start(bf16[32,2,6144]{2,1,0:T(2,128)(2,1)} %reshape.920), calls=%async_computation.2 | async-start | bytes 1572864 | tf_op jit(solution)/shard_map/all_to_all | solution.py:123
  124.6 5.1 %all-gather.6.cloned.1.call-done = bf16[24,64,1024]{2,1,0:T(8,128)(2,1)} async-done(((bf16[6,64,1024]{2,1,0:T(8,128)(2,1)}), bf16[24,64,1024]{2,1,0:T(8,128)(2,1)}) %all-gather.6.cloned.1.call-update) | async-done | bytes 3145744 | tf_op jit(solution)/shard_map/all_gather | solution.py:143
  145.8 3.0 copy.89
  148.9 3.6 subtract_convert_fusion
  153.5 2.7 convert_element_type.208
  156.2 2.8 copy.73
  159.0 3.9 reshape.924
  162.9 7.6 %all-to-all-start = ((bf16[32,2,6144]{2,1,0:T(2,128)(2,1)}), bf16[32,2,6144]{2,1,0:T(2,128)(2,1)}, u32[]{:S(2)}, u32[]{:S(2)}) async-start(bf16[32,2,6144]{2,1,0:T(2,128)(2,1)} %reshape.924), calls=%async_computation | async-start | bytes 1572864 | tf_op jit(solution)/shard_map/all_to_all | solution.py:121
  173.2 2.7 convert_element_type.209
  175.9 2.8 copy.76
  178.7 3.8 reshape.922
  182.5 4.0 all-to-all-done
  186.5 5.8 %all-to-all-start.1 = ((bf16[32,2,6144]{2,1,0:T(2,128)(2,1)}), bf16[32,2,6144]{2,1,0:T(2,128)(2,1)}, u32[]{:S(2)}, u32[]{:S(2)}) async-start(bf16[32,2,6144]{2,1,0:T(2,128)(2,1)} %reshape.922), calls=%async_computation.1 | async-start | bytes 1572864 | tf_op jit(solution)/shard_map/all_to_all | solution.py:122
  200.0 3.0 reshape.925
  206.4 6.7 %all-to-all-done.1 = bf16[32,2,6144]{2,1,0:T(2,128)(2,1)} async-done(((bf16[32,2,6144]{2,1,0:T(2,128)(2,1)}), bf16[32,2,6144]{2,1,0:T(2,128)(2,1)}, u32[]{:S(2)}, u32[]{:S(2)}) %all-to-all-start.1) | async-done | bytes 786464 | tf_op jit(solution)/shard_map/all_to_all | solution.py:122
  213.1 3.0 reshape.923
  219.8 10.8 %fusion.86 = (f32[3,512]{1,0:T(4,128)S(1)}, f32[3,512,2048]{2,1,0:T(8,128)}) fusion(pred[512,2048]{1,0:T(8,128)(4,1)} %iota_compare_fusion.3, bf16[3,2048,64]{1,2,0:T(8,128)(2,1)} %reshape.843, bf16[1,3,2048,64]{2,3,1,0:T(8,128)(2,1)} %all_to_all.49), kind=kOutput, calls=%fused_computation.153 | convolution fusion | flops 415238144 | bytes 14620672 | tf_op jit(solution)/shard_map/sub | solution.py:52
  230.5 10.1 %fusion.85 = (f32[3,512]{1,0:T(4,128)S(1)}, f32[3,512,2048]{2,1,0:T(8,128)}) fusion(pred[512,2048]{1,0:T(8,128)(4,1)S(1)} %copy-done.23, bf16[3,2048,64]{1,2,0:T(8,128)(2,1)} %reshape.843, bf16[1,3,2048,64]{2,3,1,0:T(8,128)(2,1)S(1)} %copy-done.27), kind=kOutput, calls=%fused_computation.152 | convolution fusion | flops 415238144 | bytes 14620672 | tf_op jit(solution)/shard_map/sub | solution.py:52
  240.7 10.3 %fusion.84 = (f32[3,512]{1,0:T(4,128)S(1)}, f32[3,512,2048]{2,1,0:T(8,128)}) fusion(pred[512,2048]{1,0:T(8,128)(4,1)S(1)} %copy-done.24, bf16[3,2048,64]{1,2,0:T(8,128)(2,1)} %reshape.843, bf16[1,3,2048,64]{2,3,1,0:T(8,128)(2,1)S(1)} %copy-done.27), kind=kOutput, calls=%fused_computation.151 | convolution fusion | flops 415238144 | bytes 14620672 | tf_op jit(solution)/shard_map/sub | solution.py:52
  251.0 10.0 %fusion.83 = (f32[3,512]{1,0:T(4,128)S(1)}, f32[3,512,2048]{2,1,0:T(8,128)}) fusion(pred[512,2048]{1,0:T(8,128)(4,1)S(1)} %copy-done.25, bf16[3,2048,64]{1,2,0:T(8,128)(2,1)} %reshape.843, bf16[1,3,2048,64]{2,3,1,0:T(8,128)(2,1)S(1)} %copy-done.27), kind=kOutput, calls=%fused_computation.150 | convolution fusion | flops 415238144 | bytes 14620672 | tf_op jit(solution)/shard_map/sub | solution.py:52
  261.0 6.7 %fusion.61 = bf16[1,3,512,64]{2,3,1,0:T(8,128)(2,1)S(1)} fusion(bf16[3,2048,64]{1,2,0:T(8,128)(2,1)S(1)} %copy-done.26, f32[3,512,2048]{2,1,0:T(8,128)} %get-tuple-element.43, f32[3,512]{1,0:T(4,128)S(1)} %get-tuple-element.42), kind=kOutput, calls=%fused_computation.91 | convolution fusion | flops 409042944 | bytes 13572096 | tf_op jit(solution)/shard_map/bnij,bnjd->bnid/dot_general | solution.py:54
  267.7 6.8 %fusion.62 = bf16[1,3,512,64]{2,3,1,0:T(8,128)(2,1)S(1)} fusion(bf16[3,2048,64]{1,2,0:T(8,128)(2,1)S(1)} %copy-done.26, f32[3,512,2048]{2,1,0:T(8,128)} %get-tuple-element.41, f32[3,512]{1,0:T(4,128)S(1)} %get-tuple-element.40), kind=kOutput, calls=%fused_computation.92 | convolution fusion | flops 409042944 | bytes 13572096 | tf_op jit(solution)/shard_map/bnij,bnjd->bnid/dot_general | solution.py:54
  274.6 6.8 %fusion.63 = bf16[1,3,512,64]{2,3,1,0:T(8,128)(2,1)S(1)} fusion(bf16[3,2048,64]{1,2,0:T(8,128)(2,1)S(1)} %copy-done.26, f32[3,512,2048]{2,1,0:T(8,128)} %get-tuple-element.39, f32[3,512]{1,0:T(4,128)S(1)} %get-tuple-element.38), kind=kOutput, calls=%fused_computation.93 | convolution fusion | flops 409042944 | bytes 13572096 | tf_op jit(solution)/shard_map/bnij,bnjd->bnid/dot_general | solution.py:54
  287.8 5.8 %all-to-all-start.3 = ((bf16[32,2,6144]{2,1,0:T(2,128)(2,1)}), bf16[32,2,6144]{2,1,0:T(2,128)(2,1)S(1)}, u32[]{:S(2)}, u32[]{:S(2)}) async-start(bf16[32,2,6144]{2,1,0:T(2,128)(2,1)} %reshape.926), calls=%async_computation.3 | async-start | bytes 1572864 | tf_op jit(solution)/shard_map/all_to_all | solution.py:126
  304.4 3.5 all-to-all-done.3
  318.5 8.3 %fusion.80 = (bf16[32,32,1408]{2,1,0:T(8,128)(2,1)}, bf16[32,32,1408]{2,1,0:T(8,128)(2,1)}, bf16[32,32,1408]{2,1,0:T(8,128)(2,1)}, bf16[32,32,1408]{2,1,0:T(8,128)(2,1)}) fusion(bf16[128,32,2432]{2,1,0:T(8,128)(2,1)} %bitcast.180), kind=kLoop, calls=%fused_computation.147 | loop fusion | bytes 23068672 | tf_op jit(solution)/shard_map/slice | solution.py:33
  326.8 5.7 %fusion.79 = (bf16[32,32,768]{2,1,0:T(8,128)(2,1)}, bf16[32,32,768]{2,1,0:T(8,128)(2,1)}, bf16[32,32,768]{2,1,0:T(8,128)(2,1)}, bf16[32,32,768]{2,1,0:T(8,128)(2,1)}) fusion(bf16[128,32,2432]{2,1,0:T(8,128)(2,1)} %bitcast.181), kind=kLoop, calls=%fused_computation.146 | loop fusion | bytes 12582912 | tf_op jit(solution)/shard_map/slice | solution.py:33
  334.4 4.7 %copy.84 = bf16[1024,1408]{0,1:T(8,128)(2,1)} copy(bf16[1024,1408]{1,0:T(8,128)(2,1)} %bitcast.185) | data formatting | bytes 5767168 | tf_op jit(solution)/shard_map/squeeze | solution.py:33
  339.1 4.7 %copy.85 = bf16[1024,1408]{0,1:T(8,128)(2,1)} copy(bf16[1024,1408]{1,0:T(8,128)(2,1)} %bitcast.184) | data formatting | bytes 5767168 | tf_op jit(solution)/shard_map/squeeze | solution.py:33
  345.6 3.1 fusion.91
  348.7 3.0 fusion.92
  351.8 4.9 %copy.86 = bf16[1024,1408]{0,1:T(8,128)(2,1)} copy(bf16[1024,1408]{1,0:T(8,128)(2,1)} %bitcast.183) | data formatting | bytes 5767168 | tf_op jit(solution)/shard_map/squeeze | solution.py:33
  356.7 4.9 %fusion.93 = f32[384,16,88]{0,2,1:T(8,128)} fusion(bf16[384,1024,1]{1,0,2:T(8,128)(2,1)S(1)} %bitcast.220, bf16[16,88,1024]{2,1,0:T(8,128)(2,1)} %bitcast.204), kind=kOutput, calls=%fused_computation.160 | convolution fusion | flops 1107296256 | bytes 5832704 | tf_op jit(solution)/shard_map/dot_general | solution.py:33
  361.6 4.7 %copy.87 = bf16[1024,1408]{0,1:T(8,128)(2,1)} copy(bf16[1024,1408]{1,0:T(8,128)(2,1)} %bitcast.182) | data formatting | bytes 5767168 | tf_op jit(solution)/shard_map/squeeze | solution.py:33
  366.3 3.7 fusion.94
  371.6 3.4 copy.92
  375.0 4.1 %pad.9.clone = bf16[384,32,96]{2,1,0:T(8,128)(2,1)} pad(bf16[384,32,88]{2,1,0:T(8,128)(2,1)} %copy.92, bf16[]{:T(256)} %constant.64.clone.1), padding=0_0x0_0x0_8 | pad | bytes 4521986 | tf_op jit(solution)/shard_map/jit(_pad)/pad | solution.py:135
  379.1 6.9 %dot_general.133 = bf16[6,64,3072]{2,1,0:T(8,128)(2,1)} reshape(bf16[384,32,96]{2,1,0:T(8,128)(2,1)} %pad.9.clone) | data formatting | bytes 4718592 | tf_op jit(solution)/shard_map/dot_general | solution.py:33
  386.0 3.9 reshape.912
  391.5 3.0 fusion.95
  398.0 3.8 fusion.97
  403.4 3.0 fusion.98
  (185 shorter events, 98.0 us)
Async XLA Ops:
  7.2 87.6 %copy-start = (s32[24]{0:T(128)S(1)}, s32[24]{0:T(128)}, u32[]{:S(2)}) copy-start(s32[24]{0:T(128)} %param.14) | copy-start | bytes 292
  7.2 76.4 %all-gather.8.cloned.1.call-start = ((), (), s32[]{:S(2)}) async-start(), calls=%async_computation.5 | async-start | bytes 6340608 | tf_op jit(solution)/shard_map/all_gather | solution.py:63
  8.8 121.0 %all-gather.6.cloned.1.call-start = ((), (), s32[]{:S(2)}) async-start(), calls=%async_computation.4 | async-start | bytes 3932160 | tf_op jit(solution)/shard_map/all_gather | solution.py:143
  83.6 4.5 %copy-start.41 = (bf16[4096,768]{1,0:T(8,128)(2,1)S(1)}, bf16[4096,768]{1,0:T(8,128)(2,1)}, u32[]{:S(2)}) copy-start(bf16[4096,768]{1,0:T(8,128)(2,1)} %all-gather.8.cloned.1.call-done) | copy-start | bytes 18874372
  89.7 2.9 copy-start.33
  89.7 3.0 copy-start.32
  89.7 3.0 copy-start.35
  92.5 1.5 copy-start.2
  92.6 224.1 %all-gather.10.cloned.1.call-start = ((), (), s32[]{:S(2)}) async-start(), calls=%async_computation.6 | async-start | bytes 20078592 | tf_op jit(solution)/shard_map/all_gather | solution.py:93
  119.2 13.4 %copy-start.36 = (f32[1024]{0:T(1024)S(1)}, f32[1024]{0:T(1024)}, u32[]{:S(2)}) copy-start(f32[1024]{0:T(1024)} %param.15) | copy-start | bytes 12292
  119.2 43.7 %all-to-all-start.2 = ((bf16[32,2,6144]{2,1,0:T(2,128)(2,1)}), bf16[32,2,6144]{2,1,0:T(2,128)(2,1)S(1)}, u32[]{:S(2)}, u32[]{:S(2)}) async-start(bf16[32,2,6144]{2,1,0:T(2,128)(2,1)} %reshape.920), calls=%async_computation.2 | async-start | bytes 1572864 | tf_op jit(solution)/shard_map/all_to_all | solution.py:123
  142.3 2.1 copy-start.4
  145.8 3.1 copy-start.30
  145.8 3.1 copy-start.31
  158.9 11.5 %copy-start.38 = (s32[6]{0:T(128)S(1)}, s32[6]{0:T(128)}, u32[]{:S(2)}) copy-start(s32[6]{0:T(128)} %gather_fusion.1) | copy-start | bytes 76
  158.9 11.5 %copy-start.39 = (s32[6]{0:T(128)S(1)}, s32[6]{0:T(128)}, u32[]{:S(2)}) copy-start(s32[6]{0:T(128)} %gather_fusion.3) | copy-start | bytes 76
  158.9 13.2 %copy-start.21 = (bf16[384,16,32]{0,2,1:T(8,128)(2,1)S(1)}, bf16[384,16,32]{0,2,1:T(8,128)(2,1)}, u32[]{:S(2)}) copy-start(bf16[384,16,32]{0,2,1:T(8,128)(2,1)} %get-tuple-element.28) | copy-start | bytes 1179652
  158.9 13.2 %copy-start.22 = (bf16[384,16,32]{0,2,1:T(8,128)(2,1)S(1)}, bf16[384,16,32]{0,2,1:T(8,128)(2,1)}, u32[]{:S(2)}) copy-start(bf16[384,16,32]{0,2,1:T(8,128)(2,1)} %get-tuple-element.29) | copy-start | bytes 1179652
  162.9 23.6 %all-to-all-start = ((bf16[32,2,6144]{2,1,0:T(2,128)(2,1)}), bf16[32,2,6144]{2,1,0:T(2,128)(2,1)}, u32[]{:S(2)}, u32[]{:S(2)}) async-start(bf16[32,2,6144]{2,1,0:T(2,128)(2,1)} %reshape.924), calls=%async_computation | async-start | bytes 1572864 | tf_op jit(solution)/shard_map/all_to_all | solution.py:121
  186.5 26.6 %all-to-all-start.1 = ((bf16[32,2,6144]{2,1,0:T(2,128)(2,1)}), bf16[32,2,6144]{2,1,0:T(2,128)(2,1)}, u32[]{:S(2)}, u32[]{:S(2)}) async-start(bf16[32,2,6144]{2,1,0:T(2,128)(2,1)} %reshape.922), calls=%async_computation.1 | async-start | bytes 1572864 | tf_op jit(solution)/shard_map/all_to_all | solution.py:122
  219.7 10.8 %copy-start.23 = (pred[512,2048]{1,0:T(8,128)(4,1)S(1)}, pred[512,2048]{1,0:T(8,128)(4,1)}, u32[]{:S(2)}) copy-start(pred[512,2048]{1,0:T(8,128)(4,1)} %iota_compare_fusion.2) | copy-start | bytes 3145732
  219.7 10.8 %copy-start.27 = (bf16[1,3,2048,64]{2,3,1,0:T(8,128)(2,1)S(1)}, bf16[1,3,2048,64]{2,3,1,0:T(8,128)(2,1)}, u32[]{:S(2)}) copy-start(bf16[1,3,2048,64]{2,3,1,0:T(8,128)(2,1)} %all_to_all.49) | copy-start | bytes 2359300
  230.5 10.1 %copy-start.24 = (pred[512,2048]{1,0:T(8,128)(4,1)S(1)}, pred[512,2048]{1,0:T(8,128)(4,1)}, u32[]{:S(2)}) copy-start(pred[512,2048]{1,0:T(8,128)(4,1)} %iota_compare_fusion.1) | copy-start | bytes 3145732
  240.7 10.3 %copy-start.25 = (pred[512,2048]{1,0:T(8,128)(4,1)S(1)}, pred[512,2048]{1,0:T(8,128)(4,1)}, u32[]{:S(2)}) copy-start(pred[512,2048]{1,0:T(8,128)(4,1)} %iota_compare_fusion) | copy-start | bytes 3145732
  251.0 10.0 %copy-start.26 = (bf16[3,2048,64]{1,2,0:T(8,128)(2,1)S(1)}, bf16[3,2048,64]{1,2,0:T(8,128)(2,1)}, u32[]{:S(2)}) copy-start(bf16[3,2048,64]{1,2,0:T(8,128)(2,1)} %reshape.846) | copy-start | bytes 2359300
  267.7 13.7 %slice-start = ((s8[12582912]{0:T(1024)(128)(4,1)}), s8[4194304]{0:T(1024)(128)(4,1)S(1)}, s32[]{:S(2)}) async-start(s8[12582912]{0:T(1024)(128)(4,1)} %bitcast.222), calls=%async_computation.7 | async-start | bytes 8388608
  267.7 13.7 %slice-start.1 = ((s8[12582912]{0:T(1024)(128)(4,1)}), s8[4194304]{0:T(1024)(128)(4,1)S(1)}, s32[]{:S(2)}) async-start(s8[12582912]{0:T(1024)(128)(4,1)} %bitcast.222), calls=%async_computation.8 | async-start | bytes 8388608
  274.5 6.9 %slice-start.2 = ((s8[12582912]{0:T(1024)(128)(4,1)}), s8[4194304]{0:T(1024)(128)(4,1)S(1)}, s32[]{:S(2)}) async-start(s8[12582912]{0:T(1024)(128)(4,1)} %bitcast.222), calls=%async_computation.9 | async-start | bytes 8388608
  285.3 8.2 %copy-start.40 = (s32[64]{0:T(128)S(1)}, s32[64]{0:T(128)}, u32[]{:S(2)}) copy-start(s32[64]{0:T(128)} %get-tuple-element.44) | copy-start | bytes 772
  287.8 20.1 %all-to-all-start.3 = ((bf16[32,2,6144]{2,1,0:T(2,128)(2,1)}), bf16[32,2,6144]{2,1,0:T(2,128)(2,1)S(1)}, u32[]{:S(2)}, u32[]{:S(2)}) async-start(bf16[32,2,6144]{2,1,0:T(2,128)(2,1)} %reshape.926), calls=%async_computation.3 | async-start | bytes 1572864 | tf_op jit(solution)/shard_map/all_to_all | solution.py:126
  333.3 10.5 %copy-start.8 = (f32[6,64,256]{2,1,0:T(8,128)}, f32[6,64,256]{2,1,0:T(8,128)S(1)}, u32[]{:S(2)}) copy-start(f32[6,64,256]{2,1,0:T(8,128)S(1)} %fusion.88) | copy-start | bytes 1179652
  333.7 10.1 %copy-start.10 = (f32[6,64,256]{2,1,0:T(8,128)}, f32[6,64,256]{2,1,0:T(8,128)S(1)}, u32[]{:S(2)}) copy-start(f32[6,64,256]{2,1,0:T(8,128)S(1)} %fusion.89) | copy-start | bytes 1179652
  334.1 9.7 %copy-start.12 = (f32[6,64,256]{2,1,0:T(8,128)}, f32[6,64,256]{2,1,0:T(8,128)S(1)}, u32[]{:S(2)}) copy-start(f32[6,64,256]{2,1,0:T(8,128)S(1)} %fusion.90) | copy-start | bytes 1179652
  339.1 4.7 %copy-start.37 = (f32[1024]{0:T(1024)S(1)}, f32[1024]{0:T(1024)}, u32[]{:S(2)}) copy-start(f32[1024]{0:T(1024)} %param.16) | copy-start | bytes 12292
  343.8 1.8 copy-start.14
  345.6 3.1 copy-start.15
  366.3 3.7 copy-start.17
  366.3 3.7 copy-start.18
  366.3 3.8 copy-start.19
  386.0 3.9 copy-start.7
  391.5 3.1 copy-start.16
  391.5 3.3 copy-start.20
  398.0 3.8 copy-start.5
  403.3 3.1 copy-start.9
  403.3 3.1 copy-start.11
  403.3 3.1 copy-start.13
  403.3 3.1 copy-start.28
  403.4 3.1 copy-start.29
  (4 other events, 4.8 us)
Sparse Core Ops, SparseCore 0:
  11.7 71.8 all-gather.7
  92.7 36.9 all-gather.5
  132.7 100.0 all-gather.9
where the time goes:
time: 423 us; the launch traced here: 414 us
  local copies, waits for them, and re-layouts  145 us (34%)
  matrix products  106 us (25%)
  waiting for transfers between devices  91.3 us (22%)
  other arithmetic  32.6 us (8%)
  starting transfers between devices  24.7 us (6%)
  between operations  14.8 us (3%)
    all_gather x1, waiting for transfers between devices, gather_weights(): whole = lax.all_gather(piece[None], ('req', 'seq'), axis=0, tiled=True)  72 us
    dot_general x20, matrix products, apply(): jnp.dot(inputs, gathered[r], preferred_element_type=jnp.float32)  42.4 us
    sub x4, matrix products, attend(): expo = jnp.exp(scores - top)  41.2 us
    unnamed x99, local copies, waits for them, and re-layouts  29.9 us
    squeeze x8, local copies, waits for them, and re-layouts, apply(): gathered[r]  27.7 us
    dot_general x4, matrix products, attend(): jnp.einsum('bnij,bnjd->bnid', probs, values, preferred_element_type=jnp.f...  22.8 us
    slice x3, local copies, waits for them, and re-layouts, apply(): gathered[r]  15.8 us
  transfers between devices with their start and end apart: 7, of which 5 were waited for; matrix products, arithmetic and copies ran while one was open for 43% of the time, Pallas kernels for 0%

commit v1 on v0

--- a/solution.py
+++ b/solution.py
@@ -2,6 +2,8 @@
 import jax.numpy as jnp
 from jax import lax
 from jax.sharding import PartitionSpec as P
+from jax.experimental import pallas as pl
+from jax.experimental.pallas import tpu as pltpu
 
 HEADS = 16
 HD = 64
@@ -35,25 +37,65 @@
     )
 
 
-def attend(items):
-    query, keys, values = items
-    length = query.shape[2]
-    block = min(512, length)
+Q_ROWS = 256
+K_ROWS = 256
+
+
+def attention_kernel(q_ref, k_ref, v_ref, o_ref):
+    block = pl.program_id(1)
+    query = q_ref[...].reshape(Q_ROWS, HD)
     scale = HD ** (-0.5)
-    pieces = []
-    for start in range(0, length, block):
-        q_block = query[:, :, start : start + block]
-        scores = (
-            jnp.einsum("bnid,bnjd->bnij", q_block, keys, preferred_element_type=jnp.float32) * scale
-        )
-        causal = jnp.arange(length)[None, :] <= (start + jnp.arange(block))[:, None]
-        scores = jnp.where(causal[None, None], scores, -1e30)
-        top = jnp.max(scores, axis=-1, keepdims=True)
-        expo = jnp.exp(scores - top)
-        probs = (expo / jnp.sum(expo, axis=-1, keepdims=True)).astype(jnp.bfloat16)
-        out = jnp.einsum("bnij,bnjd->bnid", probs, values, preferred_element_type=jnp.float32)
-        pieces.append(out.astype(jnp.bfloat16))
-    return jnp.concatenate(pieces, axis=2)
+    rows = block * Q_ROWS + lax.broadcasted_iota(jnp.int32, (Q_ROWS, K_ROWS), 0)
+    steps = (block + 1) * (Q_ROWS // K_ROWS)
+
+    def scores(step):
+        keys = k_ref[pl.ds(step * (K_ROWS // 64), K_ROWS // 64)].reshape(K_ROWS, HD)
+        raw = lax.dot_general(query, keys, (((1,), (1,)), ((), ())), preferred_element_type=jnp.float32)
+        cols = step * K_ROWS + lax.broadcasted_iota(jnp.int32, (Q_ROWS, K_ROWS), 1)
+        return jnp.where(cols <= rows, raw * scale, -1e30)
+
+    def first(step, carry):
+        top, total = carry
+        s = scores(step)
+        new_top = jnp.maximum(top, jnp.max(s, axis=1, keepdims=True))
+        total = total * jnp.exp(top - new_top) + jnp.sum(jnp.exp(s - new_top), axis=1, keepdims=True)
+        return new_top, total
+
+    top, total = lax.fori_loop(
+        0,
+        steps,
+        first,
+        (jnp.full((Q_ROWS, 1), -jnp.inf, jnp.float32), jnp.zeros((Q_ROWS, 1), jnp.float32)),
+    )
+
+    def second(step, acc):
+        probs = (jnp.exp(scores(step) - top) / total).astype(jnp.bfloat16)
+        values = v_ref[pl.ds(step * (K_ROWS // 64), K_ROWS // 64)].reshape(K_ROWS, HD)
+        return acc + jnp.dot(probs, values, preferred_element_type=jnp.float32)
+
+    acc = lax.fori_loop(0, steps, second, jnp.zeros((Q_ROWS, HD), jnp.float32))
+    o_ref[...] = acc.astype(o_ref.dtype).reshape(o_ref.shape)
+
+
+def attend(received):
+    sources, _, pairs, tok, _ = received.shape
+    per_block = Q_ROWS // tok
+    return pl.pallas_call(
+        attention_kernel,
+        grid=(pairs, sources // per_block),
+        in_specs=[
+            pl.BlockSpec((per_block, None, None, tok, HD), lambda p, b: (b, 0, p, 0, 0)),
+            pl.BlockSpec((sources, None, None, tok, HD), lambda p, b: (0, 1, p, 0, 0)),
+            pl.BlockSpec((sources, None, None, tok, HD), lambda p, b: (0, 2, p, 0, 0)),
+        ],
+        out_specs=pl.BlockSpec((per_block, None, tok, HD), lambda p, b: (b, p, 0, 0)),
+        out_shape=jax.ShapeDtypeStruct((sources, pairs, tok, HD), jnp.bfloat16),
+        cost_estimate=pl.CostEstimate(
+            flops=4 * pairs * sources * tok * sources * tok * HD // 2 * 2,
+            transcendentals=2 * pairs * (sources * tok) ** 2 // 2,
+            bytes_accessed=4 * pairs * sources * tok * HD * 2,
+        ),
+    )(received, received, received)
 
 
 def gather_weights(piece, rows=None):
@@ -114,16 +156,12 @@
 
     def to_pairs(array):
         paired = array.reshape(count, tok, HEADS, HD).transpose(0, 2, 1, 3)
-        return paired.reshape(groups, per_device, tok, HD)
-
-    gathered = attend(
-        (
-            lax.all_to_all(to_pairs(query), "seq", split_axis=0, concat_axis=2, tiled=True),
-            lax.all_to_all(to_pairs(keys), "seq", split_axis=0, concat_axis=2, tiled=True),
-            lax.all_to_all(to_pairs(values), "seq", split_axis=0, concat_axis=2, tiled=True),
-        )
-    )
-    returned = lax.all_to_all(gathered, "seq", split_axis=2, concat_axis=0, tiled=True)
+        return paired.reshape(groups, 1, per_device, tok, HD)
+
+    sent = jnp.concatenate([to_pairs(query), to_pairs(keys), to_pairs(values)], axis=1)
+    received = lax.all_to_all(sent, "seq", split_axis=0, concat_axis=0, tiled=True)
+    gathered = attend(received)
+    returned = lax.all_to_all(gathered, "seq", split_axis=0, concat_axis=0, tiled=True)
     attended = (
         returned.reshape(count, HEADS, tok, HD).transpose(0, 2, 1, 3).reshape(count * tok, width)
     )

time: 423 us -> 458 us (1.083)
  Pallas kernels: 0 us -> 82.3 us
  matrix products: 106 us -> 38.2 us
  waiting for transfers between devices: 91.3 us -> 148 us
  local copies, waits for them, and re-layouts: 145 us -> 120 us
  other arithmetic: 32.6 us -> 27.9 us
    pallas_call x0 -> x1, Pallas kernels: none -> 82.3 us  [attend(): pl.pallas_call(attention_kernel, grid=(pairs, sources // per_block), in_s...]
    all_to_all x4 -> x2, waiting for transfers between devices: 14.2 us -> 56.7 us  [the longest x1 48.5 us: local(): lax.all_to_all(sent, 'seq', split_axis=0, concat_axis=0, tiled=True)]
    sub x4 -> x0, matrix products: 41.2 us -> none  [attend(): expo = jnp.exp(scores - top)]
    dot_general x4 -> x0, matrix products: 22.8 us -> none  [attend(): jnp.einsum('bnij,bnjd->bnid', probs, values, preferred_element_type=jnp.f...]
    all_gather x1, waiting for transfers between devices: 5.11 us -> 19.3 us  [local(): everyone = lax.all_gather(later, 'req', axis=0, tiled=True)]
    all_to_all x6 -> x0, local copies, waits for them, and re-layouts: 11.5 us -> none  [the longest x2 5.3 us: local(): lax.all_to_all(gathered, 'seq', split_axis=2, concat_axis=0, tiled=True)]
    le x4 -> x0, other arithmetic: 6.46 us -> none  [attend(): causal = jnp.arange(length)[None, :] <= (start + jnp.arange(block))[:, None]]
    concatenate x1, other arithmetic: 0.08 us -> 5.57 us  [local(): jnp.concatenate([to_pairs(query), to_pairs(keys), to_pairs(values)], axis=1)]
  transfers between devices with their start and end apart: 7 -> 5, of which waited for: 5 -> 4; matrix products, arithmetic and copies ran while one was open for 43% -> 18% of each run, Pallas kernels for 0% -> 18%
where the time goes in v1:
time: 458 us; the launch traced here: 453 us
  waiting for transfers between devices  148 us (32%)
  local copies, waits for them, and re-layouts  120 us (26%)
  Pallas kernels  82.3 us (18%)
  matrix products  38.2 us (8%)
  other arithmetic  27.9 us (6%)
  starting transfers between devices  22.1 us (5%)
  between operations  14.6 us (3%)
    pallas_call x1, Pallas kernels, attend(): pl.pallas_call(attention_kernel, grid=(pairs, sources // per_block), in_s...  82.3 us
    all_gather x1, waiting for transfers between devices, gather_weights(): whole = lax.all_gather(piece[None], ('req', 'seq'), axis=0, tiled=True)  72 us
    all_to_all x1, waiting for transfers between devices, local(): lax.all_to_all(sent, 'seq', split_axis=0, concat_axis=0, tiled=True)  48.5 us
    dot_general x20, matrix products, apply(): jnp.dot(inputs, gathered[r], preferred_element_type=jnp.float32)  38.2 us
    squeeze x8, local copies, waits for them, and re-layouts, apply(): gathered[r]  31.8 us
    unnamed x69, local copies, waits for them, and re-layouts  26.1 us
    all_gather x1, waiting for transfers between devices, local(): everyone = lax.all_gather(later, 'req', axis=0, tiled=True)  19.3 us
    slice x3, local copies, waits for them, and re-layouts, apply(): gathered[r]  15.3 us
  transfers between devices with their start and end apart: 5, of which 4 were waited for; matrix products, arithmetic and copies ran while one was open for 18% of the time, Pallas kernels for 18%

profile of v1, /device:TPU:1, one launch (start us, length us, event | category | flops | bytes accessed | tf_op | source)
XLA Modules:
  0.0 453.4 jit_solution(9594701390337958701)
XLA Ops:
  11.6 72.0 %all-gather.8.cloned.1.call-done = bf16[4096,768]{1,0:T(8,128)(2,1)} async-done(((bf16[32,768]{1,0:T(8,128)(2,1)}), bf16[4096,768]{1,0:T(8,128)(2,1)}) %all-gather.8.cloned.1.call-update) | async-done | bytes 6291472 | tf_op jit(solution)/shard_map/all_gather | solution.py:105
  83.6 2.3 fusion.9
  85.9 2.2 fusion.13
  89.7 2.8 maximum_add_fusion
  96.4 4.1 fusion.30
  100.5 2.0 copy.36
  102.5 1.9 reshape.636
  104.5 3.0 copy.40
  107.4 3.0 copy.38
  110.5 19.3 %all-gather.6.cloned.1.call-done = bf16[24,64,1024]{2,1,0:T(8,128)(2,1)} async-done(((bf16[6,64,1024]{2,1,0:T(8,128)(2,1)}), bf16[24,64,1024]{2,1,0:T(8,128)(2,1)}) %all-gather.6.cloned.1.call-update) | async-done | bytes 3145744 | tf_op jit(solution)/shard_map/all_gather | solution.py:181
  129.7 2.5 gather_fusion
  132.9 2.2 fusion.11
  135.1 2.2 fusion.15
  137.3 2.2 fusion.19
  139.4 2.2 fusion.23
  142.3 2.1 copy-done.4
  145.8 3.1 copy.47
  148.9 3.6 subtract_convert_fusion
  153.8 2.7 copy.37
  159.0 2.7 copy.39
  161.7 5.6 %pad_maximum_fusion = bf16[32,3,3,64,64]{4,3,2,1,0:T(8,128)(2,1)} fusion(bf16[32,1,3,64,64]{4,3,2,1,0:T(8,128)(2,1)} %bitcast.97, bf16[32,1,3,64,64]{4,3,2,1,0:T(8,128)(2,1)} %bitcast.96, bf16[32,1,3,64,64]{4,3,2,1,0:T(8,128)(2,1)} %bitcast.95), kind=kLoop, calls=%fused_computation.5 | loop fusion | flops 2359296 | bytes 4718592 | tf_op jit(solution)/shard_map/concatenate | solution.py:161
  167.2 8.3 %reshape.708 = bf16[32,2,18432]{2,1,0:T(2,128)(2,1)} reshape(bf16[32,3,3,64,64]{4,3,2,1,0:T(8,128)(2,1)} %pad_maximum_fusion) | data formatting | bytes 4718592
  175.6 15.0 %all-to-all-start = ((bf16[32,2,18432]{2,1,0:T(2,128)(2,1)}), bf16[32,2,18432]{2,1,0:T(2,128)(2,1)S(1)}, u32[]{:S(2)}, u32[]{:S(2)}) async-start(bf16[32,2,18432]{2,1,0:T(2,128)(2,1)} %reshape.708), calls=%async_computation | async-start | bytes 4718592 | tf_op jit(solution)/shard_map/all_to_all | solution.py:162
  191.9 48.5 %all-to-all-done = bf16[32,2,18432]{2,1,0:T(2,128)(2,1)S(1)} async-done(((bf16[32,2,18432]{2,1,0:T(2,128)(2,1)}), bf16[32,2,18432]{2,1,0:T(2,128)(2,1)S(1)}, u32[]{:S(2)}, u32[]{:S(2)}) %all-to-all-start) | async-done | bytes 2359328 | tf_op jit(solution)/shard_map/all_to_all | solution.py:162
  240.4 4.4 reshape.709.q_ref.k_ref.v_ref
  244.9 82.3 %shard_map.121 = bf16[32,3,64,64]{3,2,1,0:T(8,128)(2,1)} custom-call(bf16[32,3,3,64,64]{4,3,2,1,0:T(8,128)(2,1)} %reshape.709.q_ref.k_ref.v_ref, bf16[32,3,3,64,64]{4,3,2,1,0:T(8,128)(2,1)} %reshape.709.q_ref.k_ref.v_ref, bf16[32,3,3,64,64]{4,3,2,1,0:T(8,128)(2,1)} %reshape.709.q_ref.k_ref.v_ref), custom_call_target="tpu_custom_call" | custom-call | flops 3221225472 | bytes 3145728 | tf_op jit(solution)/shard_map/pallas_call | solution.py:83
  327.2 3.9 reshape.710
  331.1 6.6 %all-to-all-start.1 = ((bf16[32,2,6144]{2,1,0:T(2,128)(2,1)}), bf16[32,2,6144]{2,1,0:T(2,128)(2,1)S(1)}, u32[]{:S(2)}, u32[]{:S(2)}) async-start(bf16[32,2,6144]{2,1,0:T(2,128)(2,1)} %reshape.710), calls=%async_computation.1 | async-start | bytes 1572864 | tf_op jit(solution)/shard_map/all_to_all | solution.py:164
  341.5 2.5 fusion.25
  343.9 8.1 %all-to-all-done.1 = bf16[32,2,6144]{2,1,0:T(2,128)(2,1)S(1)} async-done(((bf16[32,2,6144]{2,1,0:T(2,128)(2,1)}), bf16[32,2,6144]{2,1,0:T(2,128)(2,1)S(1)}, u32[]{:S(2)}, u32[]{:S(2)}) %all-to-all-start.1) | async-done | bytes 786464 | tf_op jit(solution)/shard_map/all_to_all | solution.py:164
  357.1 5.1 %fusion.27 = (bf16[32,32,768]{2,1,0:T(8,128)(2,1)}, bf16[32,32,768]{2,1,0:T(8,128)(2,1)}, bf16[32,32,768]{2,1,0:T(8,128)(2,1)}, bf16[32,32,768]{2,1,0:T(8,128)(2,1)S(1)}) fusion(bf16[128,32,2432]{2,1,0:T(8,128)(2,1)} %bitcast.87), kind=kLoop, calls=%fused_computation.75 | loop fusion | bytes 12582912 | tf_op jit(solution)/shard_map/slice | solution.py:35
  362.2 8.4 %fusion.28 = (bf16[32,32,1408]{2,1,0:T(8,128)(2,1)}, bf16[32,32,1408]{2,1,0:T(8,128)(2,1)}, bf16[32,32,1408]{2,1,0:T(8,128)(2,1)}, bf16[32,32,1408]{2,1,0:T(8,128)(2,1)}) fusion(bf16[128,32,2432]{2,1,0:T(8,128)(2,1)} %bitcast.88), kind=kLoop, calls=%fused_computation.76 | loop fusion | bytes 23068672 | tf_op jit(solution)/shard_map/slice | solution.py:35
  373.5 4.7 %copy.42 = bf16[1024,1408]{0,1:T(8,128)(2,1)} copy(bf16[1024,1408]{1,0:T(8,128)(2,1)} %bitcast.92) | data formatting | bytes 5767168 | tf_op jit(solution)/shard_map/squeeze | solution.py:35
  378.1 4.8 %copy.45 = bf16[1024,1408]{0,1:T(8,128)(2,1)} copy(bf16[1024,1408]{1,0:T(8,128)(2,1)} %bitcast.91) | data formatting | bytes 5767168 | tf_op jit(solution)/shard_map/squeeze | solution.py:35
  384.9 3.1 fusion.35
  388.0 3.0 fusion.38
  391.0 3.7 reshape.700
  394.7 3.7 reshape.703
  398.5 3.7 reshape.702
  403.9 4.8 %copy.44 = bf16[1024,1408]{0,1:T(8,128)(2,1)} copy(bf16[1024,1408]{1,0:T(8,128)(2,1)} %bitcast.90) | data formatting | bytes 5767168 | tf_op jit(solution)/shard_map/squeeze | solution.py:35
  408.7 4.9 %fusion.37 = f32[384,16,88]{0,2,1:T(8,128)} fusion(bf16[384,1024,1]{1,0,2:T(8,128)(2,1)S(1)} %bitcast.121, bf16[16,88,1024]{2,1,0:T(8,128)(2,1)} %bitcast.105), kind=kOutput, calls=%fused_computation.85 | convolution fusion | flops 1107296256 | bytes 5832704 | tf_op jit(solution)/shard_map/dot_general | solution.py:35
  413.6 4.7 %copy.43 = bf16[1024,1408]{0,1:T(8,128)(2,1)} copy(bf16[1024,1408]{1,0:T(8,128)(2,1)} %bitcast.89) | data formatting | bytes 5767168 | tf_op jit(solution)/shard_map/squeeze | solution.py:35
  418.3 3.7 fusion.36
  423.6 3.4 copy.49
  427.0 4.2 pad.9.clone
  431.2 5.8 %dot_general.101 = bf16[6,64,3072]{2,1,0:T(8,128)(2,1)S(1)} reshape(bf16[384,32,96]{2,1,0:T(8,128)(2,1)} %pad.9.clone) | data formatting | bytes 4718592 | tf_op jit(solution)/shard_map/dot_general | solution.py:35
  437.0 3.1 fusion.42
  442.9 2.5 fusion.39
  (127 shorter events, 38.0 us)
Async XLA Ops:
  7.2 183.4 %copy-start = (s32[24]{0:T(128)S(1)}, s32[24]{0:T(128)}, u32[]{:S(2)}) copy-start(s32[24]{0:T(128)} %param.14) | copy-start | bytes 292
  7.2 76.4 %all-gather.8.cloned.1.call-start = ((), (), s32[]{:S(2)}) async-start(), calls=%async_computation.3 | async-start | bytes 6340608 | tf_op jit(solution)/shard_map/all_gather | solution.py:105
  8.8 121.0 %all-gather.6.cloned.1.call-start = ((), (), s32[]{:S(2)}) async-start(), calls=%async_computation.2 | async-start | bytes 3932160 | tf_op jit(solution)/shard_map/all_gather | solution.py:181
  83.6 4.5 copy-start.31
  88.9 0.8 copy-start.27
  89.7 3.3 copy-start.28
  89.7 3.3 copy-start.26
  89.7 3.4 copy-start.25
  92.5 1.4 copy-start.2
  92.6 262.7 %all-gather.10.cloned.1.call-start = ((), (), s32[]{:S(2)}) async-start(), calls=%async_computation.4 | async-start | bytes 20078592 | tf_op jit(solution)/shard_map/all_gather | solution.py:135
  110.5 22.1 %copy-start.29 = (f32[1024]{0:T(1024)S(1)}, f32[1024]{0:T(1024)}, u32[]{:S(2)}) copy-start(f32[1024]{0:T(1024)} %param.15) | copy-start | bytes 12292
  142.3 2.1 copy-start.4
  175.6 64.9 %all-to-all-start = ((bf16[32,2,18432]{2,1,0:T(2,128)(2,1)}), bf16[32,2,18432]{2,1,0:T(2,128)(2,1)S(1)}, u32[]{:S(2)}, u32[]{:S(2)}) async-start(bf16[32,2,18432]{2,1,0:T(2,128)(2,1)} %reshape.708), calls=%async_computation | async-start | bytes 4718592 | tf_op jit(solution)/shard_map/all_to_all | solution.py:162
  327.2 10.7 %copy-start.22 = (bf16[384,16,32]{0,2,1:T(8,128)(2,1)S(1)}, bf16[384,16,32]{0,2,1:T(8,128)(2,1)}, u32[]{:S(2)}) copy-start(bf16[384,16,32]{0,2,1:T(8,128)(2,1)} %get-tuple-element.23) | copy-start | bytes 1179652
  331.1 21.0 %all-to-all-start.1 = ((bf16[32,2,6144]{2,1,0:T(2,128)(2,1)}), bf16[32,2,6144]{2,1,0:T(2,128)(2,1)S(1)}, u32[]{:S(2)}, u32[]{:S(2)}) async-start(bf16[32,2,6144]{2,1,0:T(2,128)(2,1)} %reshape.710), calls=%async_computation.1 | async-start | bytes 1572864 | tf_op jit(solution)/shard_map/all_to_all | solution.py:164
  371.4 0.8 copy-start.5
  371.4 1.3 copy-start.3
  371.8 1.2 copy-start.8
  372.7 0.8 copy-start.11
  378.1 4.8 %copy-start.6 = (f32[6,64,256]{2,1,0:T(8,128)S(1)}, f32[6,64,256]{2,1,0:T(8,128)}, u32[]{:S(2)}) copy-start(f32[6,64,256]{2,1,0:T(8,128)} %copy-done.5) | copy-start | bytes 1179652
  378.1 4.8 %copy-start.9 = (f32[6,64,256]{2,1,0:T(8,128)S(1)}, f32[6,64,256]{2,1,0:T(8,128)}, u32[]{:S(2)}) copy-start(f32[6,64,256]{2,1,0:T(8,128)} %copy-done.8) | copy-start | bytes 1179652
  378.1 4.8 %copy-start.30 = (f32[1024]{0:T(1024)S(1)}, f32[1024]{0:T(1024)}, u32[]{:S(2)}) copy-start(f32[1024]{0:T(1024)} %param.16) | copy-start | bytes 12292
  382.9 1.9 copy-start.13
  384.4 3.6 copy-start.23
  384.9 3.1 copy-start.14
  403.9 4.8 %copy-start.24 = (bf16[6,64,1024]{2,1,0:T(8,128)(2,1)S(1)}, bf16[6,64,1024]{2,1,0:T(8,128)(2,1)}, u32[]{:S(2)}) copy-start(bf16[6,64,1024]{2,1,0:T(8,128)(2,1)} %copy-done.23) | copy-start | bytes 2359300
  418.3 3.7 copy-start.16
  418.3 3.7 copy-start.17
  418.3 3.8 copy-start.18
  437.0 3.9 copy-start.15
  437.0 3.1 copy-start.20
  440.1 1.4 copy-start.21
  441.5 1.4 copy-start.19
  442.9 2.6 copy-start.7
  442.9 2.6 copy-start.10
  442.9 2.6 copy-start.12
  445.4 1.2 copy-start.1
Sparse Core Ops, SparseCore 0:
  11.7 71.8 all-gather.7
  92.7 36.9 all-gather.5
  132.7 110.1 all-gather.9
